TPU v7x, 512 devices: a whole 4x4x16 slice. The times are simulated.
512 devices in a mesh: row: 16 (over y, x), col: 16 (over z), depth: 2 (over core).
Axes of the slice: x: 4, y: 4, z: 16, core: 2. Of those that a mesh axis runs over, the one named last changes fastest.
Arguments:
- left_store: float32 [16, 2, 16, 2, 64, 1024], P('row', 'depth', 'col'), may hold values from -6 to 6
- left_home: int32 [16, 2, 16], P('row', 'depth'), may hold values from 0 to 15, each once within a row
- up_store: float32 [16, 2, 16, 2, 64, 1024], P('col', 'depth', 'row'), may hold values from -0.3125 to 0.3125
- up_home: int32 [16, 2, 16], P('col', 'depth'), may hold values from 0 to 15, each once within a row
- targets: int32 [16, 16, 2], P('row', 'col'), may hold values from 0 to 63, as said below
- sketch: float32 [16, 16, 2, 64, 1024], P('row', 'col'), may hold values from -0.1875 to 0.1875
Outputs:
- basis: float32 [16, 16, 2, 64, 1024], P('row', 'col', 'depth')
- weights: float32 [16, 16, 2, 64, 1024], P('row', 'col', 'depth')
Inputs may be any that keep to these rules, and one draw needn't show every extreme that they name: `left_home`: for each row and depth index the entries are the store positions 0 to 15, each once. `up_home`: for each col and depth index the entries are the store positions 0 to 15, each once. `targets`: the 2 entries of one row and col index are distinct.
All inputs are finite; a program needn't handle non-finite values.
Results may differ from a plain program's by a relative error of at most 0.0003.
Values sent between devices are 32-bit elements; how exact they have to be, the bound alone decides.
No kernel may reach another device: no remote copies, remote signals or barrier semaphores. Data moves between devices by JAX's collectives and lax.ppermute only.
A program may use at most 128 MiB of HBM per device.

v0:
```python
import math
import jax
import jax.numpy as jnp
from jax import lax
from jax.sharding import PartitionSpec as P

KD = 2
RB = 8
CB = 8


def split_up(shard, dim, devices):
    before, after = (shard.shape[:dim], shard.shape[dim + 1 :])
    return jnp.moveaxis(shard.reshape(*before, devices, -1, *after), dim, 0)


def sent_and_summed(shard, axis, dim):
    devices = lax.axis_size(axis)
    pieces = lax.all_to_all(split_up(shard, dim, devices), axis, 0, 0, tiled=True)
    return jnp.sum(pieces, axis=0)


def laid_out(pieces, dim):
    pieces = jnp.moveaxis(pieces, 0, dim)
    shape = pieces.shape
    return pieces.reshape(*shape[:dim], shape[dim] * shape[dim + 1], *shape[dim + 2 :])


def copy_for_each(shard, axis):
    devices = lax.axis_size(axis)
    return lax.all_to_all(
        jnp.broadcast_to(shard[None], (devices, *shard.shape)), axis, 0, 0, tiled=True
    )


def gathered_copies(shard, axis, dim):
    return laid_out(copy_for_each(shard, axis), dim)


def orthonormal(sample):
    gram_mat = jnp.einsum("pat,pbt->pab", sample, sample, precision=lax.Precision.HIGHEST)
    factor_low = jnp.linalg.cholesky(gram_mat)
    return lax.linalg.triangular_solve(factor_low, sample, left_side=True, lower=True)


def shards(left_store, left_home, up_store, up_home, targets, sketch):
    high = lax.Precision.HIGHEST
    left_local = left_store[0, 0]
    up_local = up_store[0, 0]
    left_table = left_home[0, 0]
    up_table = up_home[0, 0]
    left_all = lax.all_gather(left_local, "col", axis=0, tiled=True)
    up_all = lax.all_gather(up_local, "row", axis=0, tiled=True)
    left_pairs = jnp.take(left_all, left_table, axis=0)
    up_pairs = jnp.take(up_all, up_table, axis=0)
    chosen = targets[0, 0]
    block_row = chosen // CB
    block_col = chosen % CB
    row_pairs = jnp.take(left_pairs.reshape((RB, KD) + left_local.shape[1:]), block_row, axis=0)
    col_pairs = jnp.take(up_pairs.reshape((CB, KD) + up_local.shape[1:]), block_col, axis=0)
    row_basis = row_pairs[:, :, 0]
    row_coef = row_pairs[:, :, 1]
    col_coef = col_pairs[:, :, 0]
    col_basis = col_pairs[:, :, 1]
    test_rows = sketch[0, 0]
    middle = jnp.einsum("pkat,pkbt->pkab", row_coef, col_coef, precision=high)
    test_side = jnp.einsum("pat,pkbt->pkab", test_rows, col_basis, precision=high)
    folded = jnp.einsum("pkab,pkcb->pkac", test_side, middle, precision=high)
    sample_part = jnp.einsum("pkac,pkct->pat", folded, row_basis, precision=high)
    own_sketch = sent_and_summed(sample_part, "depth", 0)
    own_basis = orthonormal(own_sketch)
    bases = gathered_copies(own_basis, "depth", 0)
    inner_prod = jnp.einsum("pat,pkct->pkac", bases, row_basis, precision=high)
    turned = jnp.einsum("pkac,pkcb->pkab", inner_prod, middle, precision=high)
    project_part = jnp.einsum("pkab,pkbt->pat", turned, col_basis, precision=high)
    projected = sent_and_summed(project_part, "depth", 0)
    root_tile = math.sqrt(test_rows.shape[-1])
    return ((own_basis * root_tile)[None, None], (projected / root_tile)[None, None])


def solution(mesh):
    return jax.shard_map(
        shards,
        mesh=mesh,
        in_specs=(
            P("row", "depth", "col", None, None, None),
            P("row", "depth", None),
            P("col", "depth", "row", None, None, None),
            P("col", "depth", None),
            P("row", "col", None),
            P("row", "col", None, None, None),
        ),
        out_specs=(P("row", "col", "depth", None, None), P("row", "col", "depth", None, None)),
        check_vma=False,
    )
```

profile of v0, /device:TPU:1, one launch (start us, length us, event | category | flops | bytes accessed | tf_op | source)
XLA Modules:
  0.0 273.3 jit_solution(12288357249461976770)
XLA Ops:
  7.2 0.7 all-gather.7.cloned.1.call-update
  8.0 0.7 all-gather.5.cloned.1.call-update
  9.3 0.7 compare_and_fusion
  12.0 109.1 %all-gather.7.cloned.1.call-done = f32[16,1,1,2,64,1024]{5,4,3,2,1,0:T(8,128)} async-done(((f32[1,1,1,2,64,1024]{5,4,3,2,1,0:T(8,128)}), f32[16,1,1,2,64,1024]{5,4,3,2,1,0:T(8,128)}) %all-gather.7.cloned.1.call-update) | async-done | bytes 8388624 | tf_op jit(solution)/shard_map/all_gather | solution.py:52
  121.1 7.7 %gather_fusion.2 = f32[16,2,64,1024]{3,2,1,0:T(8,128)} fusion(f32[16,2,64,1024]{3,2,1,0:T(8,128)} %bitcast.97, s32[1024]{0:T(1024)S(1)} %pad_clamp_fusion.1), kind=kCustom, calls=%fused_computation.2.clone | custom fusion | bytes 16777280 | tf_op jit(solution)/shard_map/jit(_take)/gather | solution.py:54
  128.8 8.6 %broadcast_select_fusion = f32[16,2,64,1024]{3,2,1,0:T(8,128)} fusion(f32[16,2,64,1024]{3,2,1,0:T(8,128)} %gather_fusion.2, pred[16]{0:T(512)(128)(4,1)S(1)} %compare_and_fusion.1), kind=kLoop, calls=%fused_computation.4 | loop fusion | flops 2097152 | bytes 16777232 | tf_op jit(solution)/shard_map/jit(_take)/select_n | solution.py:54
  137.4 5.8 %gather_fusion.3 = f32[2,2,2,64,1024]{4,3,2,1,0:T(8,128)} fusion(f32[8,2,2,64,1024]{4,3,2,1,0:T(8,128)} %bitcast.94, s32[1024]{0:T(1024)S(1)} %pad_clamp_fusion), kind=kCustom, calls=%fused_computation.3.clone | custom fusion | bytes 4194312 | tf_op jit(solution)/shard_map/jit(_take)/gather | solution.py:59
  143.2 65.0 %all-gather.5.cloned.1.call-done = f32[16,1,1,2,64,1024]{5,4,3,2,1,0:T(8,128)} async-done(((f32[1,1,1,2,64,1024]{5,4,3,2,1,0:T(8,128)}), f32[16,1,1,2,64,1024]{5,4,3,2,1,0:T(8,128)}) %all-gather.5.cloned.1.call-update) | async-done | bytes 8388624 | tf_op jit(solution)/shard_map/all_gather | solution.py:53
  208.2 7.7 %gather_fusion = f32[16,2,64,1024]{3,2,1,0:T(8,128)} fusion(f32[16,2,64,1024]{3,2,1,0:T(8,128)} %bitcast.96, s32[1024]{0:T(1024)S(1)} %pad_clamp_fusion.3), kind=kCustom, calls=%fused_computation.clone | custom fusion | bytes 16777280 | tf_op jit(solution)/shard_map/jit(_take)/gather | solution.py:55
  215.8 8.6 %broadcast_select_fusion.1 = f32[16,2,64,1024]{3,2,1,0:T(8,128)} fusion(f32[16,2,64,1024]{3,2,1,0:T(8,128)} %gather_fusion, pred[16]{0:T(512)(128)(4,1)S(1)} %compare_and_fusion.3), kind=kLoop, calls=%fused_computation.5 | loop fusion | flops 2097152 | bytes 16777232 | tf_op jit(solution)/shard_map/jit(_take)/select_n | solution.py:55
  224.4 5.4 %gather_fusion.1 = f32[2,2,2,64,1024]{4,3,2,1,0:T(8,128)} fusion(f32[8,2,2,64,1024]{4,3,2,1,0:T(8,128)} %bitcast.95, s32[1024]{0:T(1024)S(1)} %pad_clamp_fusion.2), kind=kCustom, calls=%fused_computation.1.clone | custom fusion | bytes 4194312 | tf_op jit(solution)/shard_map/jit(_take)/gather | solution.py:60
  229.9 2.8 %copy_select_fusion = (f32[2,2,2,64,1024]{4,3,1,0,2:T(8,128)S(1)}, f32[2,2,2,64,1024]{4,3,1,0,2:T(8,128)S(1)}) fusion(f32[2,2,2,64,1024]{4,3,2,1,0:T(8,128)} %gather_fusion.3, pred[2]{0:T(512)(128)(4,1)S(1)} %get-tuple-element.4, f32[2,2,2,64,1024]{4,3,2,1,0:T(8,128)} %gather_fusion.1, pred[2]{0:T(512)(128)(4,1)S(1)} %get-tuple-element.8), kind=kLoop, calls=%fused_computation.6 | loop fusion | flops 1048576 | bytes 8388612 | tf_op jit(solution)/shard_map/jit(_take)/select_n | solution.py:59
  232.7 1.6 fusion.1
  234.3 1.1 fusion
  235.7 0.7 convolution_bitcast_fusion.1
  236.4 4.6 %all_to_all.15 = f32[2,1,64,1024]{3,2,1,0:T(8,128)S(1)} all-to-all(f32[2,1,64,1024]{3,2,1,0:T(8,128)S(1)} %convolution_bitcast_fusion.1), channel_id=1, replica_groups=mesh['row'=16,'col'=16,'depth'=2] {'depth'}, dimensions={0} | all-to-all | bytes 1048576 | tf_op jit(solution)/shard_map/all_to_all | solution.py:19
  241.5 5.8 %custom-call.7 = f32[1,64,64]{2,1,0:T(8,128)S(1)} custom-call(f32[1,64,64]{2,1,0:T(8,128)S(1)} %fusion.6), custom_call_target="Cholesky" | custom-call | tf_op jit(solution)/shard_map/jit(cholesky)/cholesky | solution.py:42
  248.7 4.9 %custom-call.8 = f32[1,1,64,64]{2,3,1,0:T(8,128)S(1)} custom-call(f32[1,1,64,64]{3,2,1,0:T(8,128)S(1)} %fusion.5), custom_call_target="InvertDiagBlocksLowerTriangular" | custom-call | tf_op jit(solution)/shard_map/triangular_solve | solution.py:43
  254.1 0.7 multiply_bitcast_fusion.1
  254.8 4.2 %all_to_all.16 = f32[2,1,64,1024]{3,2,1,0:T(8,128)S(1)} all-to-all(f32[2,1,64,1024]{3,2,1,0:T(8,128)S(1)} %broadcast_in_dim.33), channel_id=1, replica_groups=mesh['row'=16,'col'=16,'depth'=2] {'depth'}, dimensions={0} | all-to-all | bytes 1048576 | tf_op jit(solution)/shard_map/all_to_all | solution.py:31
  259.0 1.6 fusion.2
  260.9 0.7 convolution_bitcast_fusion
  261.6 4.2 %all_to_all.17 = f32[2,1,64,1024]{3,2,1,0:T(8,128)S(1)} all-to-all(f32[2,1,64,1024]{3,2,1,0:T(8,128)S(1)} %convolution_bitcast_fusion), channel_id=1, replica_groups=mesh['row'=16,'col'=16,'depth'=2] {'depth'}, dimensions={0} | all-to-all | bytes 1048576 | tf_op jit(solution)/shard_map/all_to_all | solution.py:19
  265.8 0.7 multiply_bitcast_fusion
  (28 shorter events, 5.7 us)
Async XLA Ops:
  7.2 225.5 %copy-start = (f32[1,1,2,64,1024]{4,3,2,1,0:T(8,128)S(1)}, f32[1,1,2,64,1024]{4,3,2,1,0:T(8,128)}, u32[]{:S(2)}) copy-start(f32[1,1,2,64,1024]{4,3,2,1,0:T(8,128)} %param.15) | copy-start | bytes 1572868
  7.2 113.9 %all-gather.7.cloned.1.call-start = ((), (), s32[]{:S(2)}) async-start(), calls=%async_computation.4 | async-start | bytes 8912896 | tf_op jit(solution)/shard_map/all_gather | solution.py:52
  7.9 200.3 %all-gather.5.cloned.1.call-start = ((), (), s32[]{:S(2)}) async-start(), calls=%async_computation.3 | async-start | bytes 8912896 | tf_op jit(solution)/shard_map/all_gather | solution.py:53
  232.6 3.1 %copy-start.1 = (f32[2,2,2,64,1024]{4,3,1,0,2:T(8,128)}, f32[2,2,2,64,1024]{4,3,1,0,2:T(8,128)S(1)}, u32[]{:S(2)}) copy-start(f32[2,2,2,64,1024]{4,3,1,0,2:T(8,128)S(1)} %get-tuple-element.10) | copy-start | bytes 6291460
  253.6 5.4 %copy-start.2 = (f32[2,2,2,64,1024]{4,3,1,0,2:T(8,128)S(1)}, f32[2,2,2,64,1024]{4,3,1,0,2:T(8,128)}, u32[]{:S(2)}) copy-start(f32[2,2,2,64,1024]{4,3,1,0,2:T(8,128)} %copy-done.1) | copy-start | bytes 6291460
Sparse Core Ops, SparseCore 0:
  10.1 110.9 all-gather.6
  124.1 84.0 all-gather.4
where the time goes:
time: 274 us; the launch traced here: 273 us
  waiting for transfers between devices  175 us (64%)
  other arithmetic  36.9 us (13%)
  local copies, waits for them, and re-layouts  26.7 us (10%)
  between operations  14.2 us (5%)
  blocking collectives  12.9 us (5%)
  matrix products  7.07 us (3%)
    all_gather x1, waiting for transfers between devices, shards(): left_all = lax.all_gather(left_local, 'col', axis=0, tiled=True)  109 us
    all_gather x1, waiting for transfers between devices, shards(): up_all = lax.all_gather(up_local, 'row', axis=0, tiled=True)  65 us
    select_n x2, other arithmetic, shards(): left_pairs = jnp.take(left_all, left_table, axis=0)  9.27 us
    select_n x2, other arithmetic, shards(): up_pairs = jnp.take(up_all, up_table, axis=0)  9.26 us
    all_to_all x2, blocking collectives, sent_and_summed(): lax.all_to_all(split_up(shard, dim, devices), axis, 0, 0, tiled=True)  8.78 us
    gather x1, local copies, waits for them, and re-layouts, shards(): left_pairs = jnp.take(left_all, left_table, axis=0)  7.68 us
    gather x1, local copies, waits for them, and re-layouts, shards(): up_pairs = jnp.take(up_all, up_table, axis=0)  7.67 us
    another operation x3, other arithmetic, orthonormal(): factor_low = jnp.linalg.cholesky(gram_mat)  6.52 us
  transfers between devices with their start and end apart: 2, of which 2 were waited for; matrix products, arithmetic and copies ran while one was open for 9% of the time, Pallas kernels for 0%

commit v1 on v0

--- a/solution.py
+++ b/solution.py
@@ -49,7 +49,10 @@
     up_local = up_store[0, 0]
     left_table = left_home[0, 0]
     up_table = up_home[0, 0]
-    left_all = lax.all_gather(left_local, "col", axis=0, tiled=True)
+    devices_2 = lax.axis_size("col")
+    tiles = jnp.stack([left_local for _ in range(devices_2)])
+    tiles = lax.all_to_all(tiles, "col", split_axis=0, concat_axis=0)
+    left_all = jnp.concatenate(tiles, axis=0)
     up_all = lax.all_gather(up_local, "row", axis=0, tiled=True)
     left_pairs = jnp.take(left_all, left_table, axis=0)
     up_pairs = jnp.take(up_all, up_table, axis=0)

time: 274 us -> 456 us (1.66)
  waiting for transfers between devices: 175 us -> 340 us
  starting transfers between devices: 0.08 us -> 16 us
  local copies, waits for them, and re-layouts: 26.7 us -> 31.7 us
    all_to_all x0 -> x1, waiting for transfers between devices: none -> 249 us  [shards(): tiles = lax.all_to_all(tiles, 'col', split_axis=0, concat_axis=0)]
    all_gather x1 -> x0, waiting for transfers between devices: 109 us -> none  [shards(): left_all = lax.all_gather(left_local, 'col', axis=0, tiled=True)]
    all_gather x1, waiting for transfers between devices: 65 us -> 90.5 us  [shards(): up_all = lax.all_gather(up_local, 'row', axis=0, tiled=True)]
    all_to_all x0 -> x1, starting transfers between devices: none -> 15.9 us  [shards(): tiles = lax.all_to_all(tiles, 'col', split_axis=0, concat_axis=0)]
    another operation x0 -> x1, local copies, waits for them, and re-layouts: none -> 5.38 us  [shards(): tiles = jnp.stack([left_local for _ in range(devices_2)])]
  transfers between devices with their start and end apart: 2 -> 2, of which waited for: 2 -> 2; matrix products, arithmetic and copies ran while one was open for 9% -> 5% of each run, Pallas kernels for 0% -> 0%
where the time goes in v1:
time: 456 us
  waiting for transfers between devices  340 us (75%)
  other arithmetic  33.6 us (7%)
  local copies, waits for them, and re-layouts  31.7 us (7%)
  starting transfers between devices  16 us (4%)
  between operations  14.3 us (3%)
  blocking collectives  13.5 us (3%)
  matrix products  7.07 us (2%)
    all_to_all x1, waiting for transfers between devices, shards(): tiles = lax.all_to_all(tiles, 'col', split_axis=0, concat_axis=0)  249 us
    all_gather x1, waiting for transfers between devices, shards(): up_all = lax.all_gather(up_local, 'row', axis=0, tiled=True)  90.5 us
    all_to_all x1, starting transfers between devices, shards(): tiles = lax.all_to_all(tiles, 'col', split_axis=0, concat_axis=0)  15.9 us
    all_to_all x2, blocking collectives, sent_and_summed(): lax.all_to_all(split_up(shard, dim, devices), axis, 0, 0, tiled=True)  9.33 us
  transfers between devices with their start and end apart: 2, of which 2 were waited for; matrix products, arithmetic and copies ran while one was open for 5% of the time, Pallas kernels for 0%

profile of v1, /device:TPU:1, one launch (start us, length us, event | category | flops | bytes accessed | tf_op | source)
XLA Modules:
  0.0 455.8 jit_solution(13733772855081996594)
XLA Ops:
  7.2 5.4 %stack.3 = f32[16,1,2,64,1024]{4,3,2,1,0:T(8,128)} broadcast(f32[2,64,1024]{2,1,0:T(8,128)} %bitcast.98), dimensions={2,3,4} | broadcast | bytes 8912896 | tf_op jit(solution)/shard_map/stack | solution.py:53
  12.6 15.9 %all-to-all-start = ((f32[16,1,2,64,1024]{4,3,2,1,0:T(8,128)}), f32[16,1,2,64,1024]{4,3,2,1,0:T(8,128)}, u32[]{:S(2)}, u32[]{:S(2)}) async-start(f32[16,1,2,64,1024]{4,3,2,1,0:T(8,128)} %stack.3), calls=%async_computation | async-start | bytes 16777216 | tf_op jit(solution)/shard_map/all_to_all | solution.py:54
  28.5 0.7 all-gather.3.cloned.1.call-update
  29.4 90.5 %all-gather.3.cloned.1.call-done = f32[16,1,1,2,64,1024]{5,4,3,2,1,0:T(8,128)} async-done(((f32[1,1,1,2,64,1024]{5,4,3,2,1,0:T(8,128)}), f32[16,1,1,2,64,1024]{5,4,3,2,1,0:T(8,128)}) %all-gather.3.cloned.1.call-update) | async-done | bytes 8388624 | tf_op jit(solution)/shard_map/all_gather | solution.py:56
  119.9 7.7 %gather_fusion = f32[16,2,64,1024]{3,2,1,0:T(8,128)} fusion(f32[16,2,64,1024]{3,2,1,0:T(8,128)} %bitcast.97, s32[1024]{0:T(1024)S(1)} %pad_clamp_fusion.3), kind=kCustom, calls=%fused_computation.clone | custom fusion | bytes 16777280 | tf_op jit(solution)/shard_map/jit(_take)/gather | solution.py:58
  127.5 8.6 %broadcast_select_fusion.1 = f32[16,2,64,1024]{3,2,1,0:T(8,128)} fusion(f32[16,2,64,1024]{3,2,1,0:T(8,128)} %gather_fusion, pred[16]{0:T(512)(128)(4,1)S(1)} %compare_and_fusion.3), kind=kLoop, calls=%fused_computation.5 | loop fusion | flops 2097152 | bytes 16777232 | tf_op jit(solution)/shard_map/jit(_take)/select_n | solution.py:58
  136.1 5.4 %gather_fusion.1 = f32[2,2,2,64,1024]{4,3,2,1,0:T(8,128)} fusion(f32[8,2,2,64,1024]{4,3,2,1,0:T(8,128)} %bitcast.95, s32[1024]{0:T(1024)S(1)} %pad_clamp_fusion.2), kind=kCustom, calls=%fused_computation.1.clone | custom fusion | bytes 4194312 | tf_op jit(solution)/shard_map/jit(_take)/gather | solution.py:63
  141.5 248.6 %all-to-all-done = f32[16,1,2,64,1024]{4,3,2,1,0:T(8,128)} async-done(((f32[16,1,2,64,1024]{4,3,2,1,0:T(8,128)}), f32[16,1,2,64,1024]{4,3,2,1,0:T(8,128)}, u32[]{:S(2)}, u32[]{:S(2)}) %all-to-all-start) | async-done | bytes 8388640 | tf_op jit(solution)/shard_map/all_to_all | solution.py:54
  390.1 7.7 %gather_fusion.2 = f32[16,2,64,1024]{3,2,1,0:T(8,128)} fusion(f32[16,2,64,1024]{3,2,1,0:T(8,128)} %bitcast.10, s32[1024]{0:T(1024)S(1)} %pad_clamp_fusion.1), kind=kCustom, calls=%fused_computation.2.clone | custom fusion | bytes 16777280 | tf_op jit(solution)/shard_map/jit(_take)/gather | solution.py:57
  397.8 8.6 %broadcast_select_fusion = f32[16,2,64,1024]{3,2,1,0:T(8,128)} fusion(f32[16,2,64,1024]{3,2,1,0:T(8,128)} %gather_fusion.2, pred[16]{0:T(512)(128)(4,1)S(1)} %compare_and_fusion.1), kind=kLoop, calls=%fused_computation.4 | loop fusion | flops 2097152 | bytes 16777232 | tf_op jit(solution)/shard_map/jit(_take)/select_n | solution.py:57
  406.4 5.4 %gather_fusion.3 = f32[2,2,2,64,1024]{4,3,2,1,0:T(8,128)} fusion(f32[8,2,2,64,1024]{4,3,2,1,0:T(8,128)} %bitcast.96, s32[1024]{0:T(1024)S(1)} %pad_clamp_fusion), kind=kCustom, calls=%fused_computation.3.clone | custom fusion | bytes 4194312 | tf_op jit(solution)/shard_map/jit(_take)/gather | solution.py:62
  411.8 2.8 copy_select_fusion
  414.6 1.6 fusion.1
  416.2 1.1 fusion
  417.7 0.7 convolution_bitcast_fusion.1
  418.3 5.2 %all_to_all.20 = f32[2,1,64,1024]{3,2,1,0:T(8,128)S(1)} all-to-all(f32[2,1,64,1024]{3,2,1,0:T(8,128)S(1)} %convolution_bitcast_fusion.1), channel_id=1, replica_groups=mesh['row'=16,'col'=16,'depth'=2] {'depth'}, dimensions={0} | all-to-all | bytes 1048576 | tf_op jit(solution)/shard_map/all_to_all | solution.py:19
  424.0 5.8 %custom-call.7 = f32[1,64,64]{2,1,0:T(8,128)S(1)} custom-call(f32[1,64,64]{2,1,0:T(8,128)S(1)} %fusion.6), custom_call_target="Cholesky" | custom-call | tf_op jit(solution)/shard_map/jit(cholesky)/cholesky | solution.py:42
  431.2 4.9 %custom-call.8 = f32[1,1,64,64]{2,3,1,0:T(8,128)S(1)} custom-call(f32[1,1,64,64]{3,2,1,0:T(8,128)S(1)} %fusion.5), custom_call_target="InvertDiagBlocksLowerTriangular" | custom-call | tf_op jit(solution)/shard_map/triangular_solve | solution.py:43
  436.5 0.7 multiply_bitcast_fusion.1
  437.3 4.2 all_to_all.21
  441.5 1.6 fusion.2
  443.4 0.7 convolution_bitcast_fusion
  444.1 4.2 all_to_all.22
  448.2 0.7 multiply_bitcast_fusion
  (34 shorter events, 3.0 us)
Async XLA Ops:
  7.2 407.4 %copy-start = (f32[1,1,2,64,1024]{4,3,2,1,0:T(8,128)S(1)}, f32[1,1,2,64,1024]{4,3,2,1,0:T(8,128)}, u32[]{:S(2)}) copy-start(f32[1,1,2,64,1024]{4,3,2,1,0:T(8,128)} %param.15) | copy-start | bytes 1572868
  12.6 16.7 %copy-start.4 = (s32[1,1,16]{2,1,0:T(1,128)S(1)}, s32[1,1,16]{2,1,0:T(1,128)}, u32[]{:S(2)}) copy-start(s32[1,1,16]{2,1,0:T(1,128)} %param.11) | copy-start | bytes 196
  12.6 16.7 %copy-start.3 = (s32[1,1,2]{2,1,0:T(1,128)S(1)}, s32[1,1,2]{2,1,0:T(1,128)}, u32[]{:S(2)}) copy-start(s32[1,1,2]{2,1,0:T(1,128)} %param.14) | copy-start | bytes 28
  12.6 16.7 %copy-start.5 = (s32[1,1,16]{2,1,0:T(1,128)S(1)}, s32[1,1,16]{2,1,0:T(1,128)}, u32[]{:S(2)}) copy-start(s32[1,1,16]{2,1,0:T(1,128)} %param.13) | copy-start | bytes 196
  12.6 377.5 %all-to-all-start = ((f32[16,1,2,64,1024]{4,3,2,1,0:T(8,128)}), f32[16,1,2,64,1024]{4,3,2,1,0:T(8,128)}, u32[]{:S(2)}, u32[]{:S(2)}) async-start(f32[16,1,2,64,1024]{4,3,2,1,0:T(8,128)} %stack.3), calls=%async_computation | async-start | bytes 16777216 | tf_op jit(solution)/shard_map/all_to_all | solution.py:54
  28.5 91.4 %all-gather.3.cloned.1.call-start = ((), (), s32[]{:S(2)}) async-start(), calls=%async_computation.4 | async-start | bytes 8912896 | tf_op jit(solution)/shard_map/all_gather | solution.py:56
  414.6 3.1 copy-start.1
  436.1 5.4 %copy-start.2 = (f32[2,2,2,64,1024]{4,3,1,0,2:T(8,128)S(1)}, f32[2,2,2,64,1024]{4,3,1,0,2:T(8,128)}, u32[]{:S(2)}) copy-start(f32[2,2,2,64,1024]{4,3,1,0,2:T(8,128)} %copy-done.1) | copy-start | bytes 6291460
Sparse Core Ops, SparseCore 0:
  32.3 87.5 all-gather.2
